TPU v7x, 32 devices: a whole 2x2x4 slice. The times are simulated.
32 devices in a mesh: wave: 16 (over z, y, x), field: 2 (over core).
Axes of the slice: x: 2, y: 2, z: 4, core: 2. Of those that a mesh axis runs over, the one named last changes fastest.
Arguments:
- right_vector: float32 [4, 3, 512, 2, 512], P('field', None, 'wave'), may hold values from -8 to 8
- left_prev: float32 [4, 3, 512, 2, 512], P('field', None, 'wave'), may hold values from -6 to 6
- beta_prev: float32 [1], replicated, may hold values from 0.5 to 2
- kept_vectors: bfloat16 [20, 4, 3, 512, 2, 512], P(None, 'field', None, 'wave'), may hold values from -8 to 8
- kept_count: int32 [1], replicated, may hold values from 1 to 20
- wave_table: int32 [512], replicated, may hold values from 0 to 511, each once
- legendre: float32 [512, 512, 512], P('wave'), may hold values from -0.25 to 0.25
- quad_weights: float32 [512], replicated, may hold values from 0.2 to 1
- coef_value: bfloat16 [3, 3, 512, 1024], P(None, None, 'wave'), may hold values from -2.390625 to 2.390625
- coef_zonal: bfloat16 [3, 3, 512, 1024], P(None, None, 'wave'), may hold values from -2.390625 to 2.390625
Outputs:
- left_vector: float32 [4, 3, 512, 2, 512], P('field', None, 'wave')
- right_next: float32 [4, 3, 512, 2, 512], P('field', None, 'wave')
- correlations: float32 [20], replicated
- norms: float32 [2], replicated
Inputs may be any that keep to these rules, and one draw needn't show every extreme that they name: The stored vectors numbered below kept_count take part. A permutation: spectral slot s holds zonal wavenumber wave_table[s].
All inputs are finite; a program needn't handle non-finite values.
Results may differ from a plain program's by a relative error of at most 0.0003.
Values sent between devices are 32-bit elements; how exact they have to be, the bound alone decides.
A program may use at most 192 MiB of HBM per device.

v0:
```python
import math
import jax
import jax.numpy as jnp
from jax import lax
from jax.sharding import PartitionSpec as P

time_step = 0.5
epsilon = 1e-06
highest = lax.Precision.HIGHEST


def fourier_tables(wave_table, longitudes, wave_count):
    column = jnp.arange(longitudes, dtype=jnp.int32)
    phase_index = wave_table[:, None] * column[None, :] % longitudes
    angle_rows = phase_index.astype(jnp.float32) * (2.0 * math.pi / longitudes)
    cosine = jnp.cos(angle_rows)
    sine_rows = jnp.sin(angle_rows)
    factor = wave_count ** (-0.5)
    slope_scale = (wave_table.astype(jnp.float32) / wave_count * factor)[:, None, None]
    value_rows = jnp.stack([cosine, -sine_rows], axis=1) * factor
    slope_rows = jnp.stack([-sine_rows, -cosine], axis=1) * slope_scale
    synthesis = jnp.stack([value_rows, slope_rows], axis=2)
    analysis = jnp.stack([cosine, -sine_rows], axis=1) * longitudes ** (-0.5)
    return (synthesis, analysis)


def body(
    right_vector,
    left_prev,
    beta_prev,
    kept_vectors,
    kept_count,
    wave_table,
    legendre,
    quad_weights,
    coef_value,
    coef_zonal,
):
    levels = right_vector.shape[0]
    fields = right_vector.shape[1]
    waves_dev = legendre.shape[0]
    degrees = legendre.shape[1]
    lat_dev = coef_value.shape[2]
    longitudes = coef_value.shape[3]
    groups = lax.axis_size("wave")
    keep_count = kept_vectors.shape[0]
    entries = float(right_vector.size * groups * lax.axis_size("field"))
    device = lax.axis_index("wave")
    own_waves = lax.dynamic_slice_in_dim(wave_table, device * waves_dev, waves_dev)
    degree_ids = jnp.arange(degrees, dtype=jnp.int32)
    live_mask = (degree_ids[None, :] >= own_waves[:, None]).astype(jnp.float32)
    wide_mask = live_mask[None, None, :, None, :]
    own_weights = lax.dynamic_slice_in_dim(quad_weights, device * lat_dev, lat_dev)[
        None, None, :, None
    ]
    synthesis, analysis = fourier_tables(wave_table, longitudes, degrees)
    synthesis = synthesis.reshape(groups, waves_dev, 2, 2, longitudes)
    analysis = analysis.reshape(groups, waves_dev, 2, longitudes)
    blocked = legendre.reshape(waves_dev, degrees, groups, lat_dev)
    value_coef = coef_value.astype(jnp.float32)
    zonal_coef = coef_zonal.astype(jnp.float32)

    def to_latitudes(spectral):
        latitude_part = jnp.einsum("lfsrn,snwt->lwftsr", spectral, blocked, precision=highest)
        return latitude_part.reshape(levels, groups, fields * lat_dev * waves_dev * 2)

    def to_degrees(gathered):
        spectral = jnp.einsum("lwftsr,snwt->lfsrn", gathered, blocked, precision=highest)
        return spectral * wide_mask

    right_live = right_vector * wide_mask
    prev_live = left_prev * wide_mask
    block_in = lax.all_to_all(
        to_latitudes(right_live), "wave", split_axis=1, concat_axis=1, tiled=True
    )
    item_count = block_in.shape[0]
    spread = block_in.reshape(item_count, groups, fields, lat_dev, waves_dev, 2)
    grid_values = jnp.einsum("iwftsr,wsrkx->ikftx", spread, synthesis, precision=highest)
    tendency = jnp.sum(value_coef[None] * grid_values[:, 0, None], axis=2)
    tendency = tendency + jnp.sum(zonal_coef[None] * grid_values[:, 1, None], axis=2)
    weighted = tendency * own_weights
    outgoing = jnp.einsum("iftx,wsrx->iwftsr", weighted, analysis, precision=highest)
    returned = lax.all_to_all(
        outgoing.reshape(item_count, groups, -1), "wave", split_axis=1, concat_axis=1, tiled=True
    )
    gathered = returned.reshape(item_count, groups, fields, lat_dev, waves_dev, 2)
    residual_left = right_live + time_step * to_degrees(gathered) - beta_prev[0] * prev_live
    kept_live = (kept_vectors.astype(jnp.float32) * wide_mask[None]).reshape(keep_count, -1)
    live_flags = (jnp.arange(keep_count, dtype=jnp.int32) < kept_count[0]).astype(jnp.float32)

    def project(vector):
        return jnp.dot(kept_live, vector.reshape(-1), precision=highest)

    block_in = lax.all_to_all(
        to_latitudes(residual_left), "wave", split_axis=1, concat_axis=1, tiled=True
    )
    item_count = block_in.shape[0]
    spread = block_in.reshape(item_count, groups, fields, lat_dev, waves_dev, 2)
    weighted = jnp.einsum("iwftsr,wsrx->iftx", spread, analysis, precision=highest) * own_weights
    value_part = jnp.sum(value_coef[None] * weighted[:, :, None], axis=1)
    zonal_part = jnp.sum(zonal_coef[None] * weighted[:, :, None], axis=1)
    stacked = jnp.stack([value_part, zonal_part], axis=1)
    outgoing = jnp.einsum("ikftx,wsrkx->iwftsr", stacked, synthesis, precision=highest)
    returned = lax.all_to_all(
        outgoing.reshape(item_count, groups, -1), "wave", split_axis=1, concat_axis=1, tiled=True
    )
    gathered = returned.reshape(item_count, groups, fields, lat_dev, waves_dev, 2)
    adjoint_raw = residual_left + time_step * to_degrees(gathered)
    totals = lax.psum(
        (
            jnp.sum(residual_left * residual_left),
            jnp.sum(adjoint_raw * adjoint_raw),
            jnp.sum(adjoint_raw * right_live),
            jnp.sum(right_live * right_live),
            project(adjoint_raw),
            project(right_live),
            jnp.dot(kept_live, kept_live.T, precision=highest),
        ),
        ("wave", "field"),
    )
    left_square, image_square, image_cross, right_square, kept_image, kept_right, gram_matrix = [
        summed / entries for summed in totals
    ]
    alpha_norm = jnp.sqrt(left_square + epsilon)
    left_vector = residual_left / alpha_norm
    raw_correlation = kept_image / alpha_norm - alpha_norm * kept_right
    correlations = raw_correlation * live_flags
    square = (
        image_square / (alpha_norm * alpha_norm)
        - 2.0 * image_cross
        + alpha_norm * alpha_norm * right_square
    )
    square = (
        square
        - 2.0 * jnp.sum(correlations * raw_correlation)
        + jnp.dot(
            correlations, jnp.dot(gram_matrix, correlations, precision=highest), precision=highest
        )
    )
    beta_norm = jnp.sqrt(square + epsilon)
    orthogonal = (
        adjoint_raw / alpha_norm
        - alpha_norm * right_live
        - jnp.dot(correlations, kept_live, precision=highest).reshape(right_live.shape)
    )
    return (left_vector, orthogonal / beta_norm, correlations, jnp.stack([alpha_norm, beta_norm]))


def solution(mesh):
    return jax.shard_map(
        body,
        mesh=mesh,
        in_specs=(
            P("field", None, "wave", None, None),
            P("field", None, "wave", None, None),
            P(),
            P(None, "field", None, "wave", None, None),
            P(),
            P(),
            P("wave", None, None),
            P(),
            P(None, None, "wave", None),
            P(None, None, "wave", None),
        ),
        out_specs=(
            P("field", None, "wave", None, None),
            P("field", None, "wave", None, None),
            P(),
            P(),
        ),
        check_vma=False,
    )
```

profile of v0, /device:TPU:0, one launch (start us, length us, event | category | flops | bytes accessed | tf_op | source)
XLA Modules:
  0.0 760.5 jit_solution(3930852589484011653)
XLA Ops:
  1.5 33.4 %copy.73 = f32[32,512,512]{1,2,0:T(8,128)} copy(f32[32,512,512]{2,1,0:T(8,128)} %param.16) | data formatting | bytes 67108864 | tf_op args[6]
  34.9 86.2 %convolution_bitcast_fusion.1 = f32[2,16,3,32,32,2]{3,2,1,5,0,4:T(4,128)} fusion(f32[32,512,16,32,1,1]{1,3,2,5,4,0:T(8,128)} %bitcast.179, f32[2,3,32,2,512]{4,3,2,1,0:T(2,128)S(1)} %copy-done.1, f32[32,512]{1,0:T(8,128)S(1)} %fusion.74), kind=kOutput, calls=%fused_computation.31 | convolution fusion | flops 1208156160 | bytes 35192832 | tf_op jit(solution)/shard_map/lfsrn,snwt->lwftsr/dot_general | solution.py:64
  121.2 9.5 %copy.74 = f32[2,16,3,32,32,2]{1,5,4,3,2,0:T(2,128)} copy(f32[2,16,3,32,32,2]{3,2,1,5,0,4:T(4,128)} %convolution_bitcast_fusion.1) | data formatting | bytes 1572864 | tf_op jit(solution)/shard_map/lfsrn,snwt->lwftsr/transpose | solution.py:64
  130.7 5.4 copy.75
  136.1 8.4 %all-to-all-start = ((f32[2,16,6144]{2,0,1:T(2,128)}), f32[2,16,6144]{2,0,1:T(2,128)}, u32[]{:S(2)}, u32[]{:S(2)}) async-start(f32[2,16,6144]{2,0,1:T(2,128)} %copy.75), calls=%async_computation | async-start | bytes 1572864 | tf_op jit(solution)/shard_map/all_to_all | solution.py:73
  146.7 10.7 %fusion.62 = (f32[16,32,1,1,1024]{4,1,0,3,2:T(8,128)S(1)}, f32[16,32,1,1,1024]{4,1,0,3,2:T(8,128)S(1)}, f32[16,32,1,1,1024]{4,1,0,2,3:T(8,128)S(1)}, f32[16,32,1...) fusion(s32[16,32]{1,0:T(8,128)S(1)} %mul.312), kind=kLoop, calls=%fused_computation.76 | loop fusion | flops 8388608 | bytes 12584960 | tf_op jit(solution)/shard_map/stack | solution.py:23
  169.1 9.6 %copy.77 = f32[2,16,3,32,32,2]{4,3,1,5,2,0:T(8,128)} copy(f32[2,16,3,32,32,2]{1,5,4,3,2,0:T(2,128)} %bitcast.187) | data formatting | bytes 1572864 | tf_op jit(solution)/shard_map/reshape | solution.py:77
  178.7 9.6 %fusion.32 = f32[2,2,3,32,1024]{4,3,2,0,1:T(8,128)S(1)} fusion(f32[2,16,3,32,32,2]{4,3,1,5,2,0:T(8,128)} %copy.77, f32[16,32,2,1,1024]{4,1,0,2,3:T(8,128)} %maximum_multiply_fusion.2, f32[16,32,2,1,1024]{4,1,0,2,3:T(8,128)} %fusion.14), kind=kOutput, calls=%fused_computation.45 | convolution fusion | flops 4833935360 | bytes 10747904 | tf_op jit(solution)/shard_map/iwftsr,wsrkx->ikftx/dot_general | solution.py:78
  190.5 11.8 %fusion.24 = f32[2,16,3,32,32,2]{3,4,2,0,5,1:T(8,128)} fusion(f32[2,3,32,1024]{3,2,1,0:T(8,128)S(1)} %get-tuple-element.46, f32[2,3,32,1024]{3,2,1,0:T(8,128)S(1)} %get-tuple-element.45, f32[32]{0:T(128)S(1)} %dynamic_slice.7, f32[16,32,1,1024]{3,1,0,2:T(8,128)S(1)} %copy-done.8, f32[16,32,1,1024]{3,1,0,2:T(8,128)S(1)} %copy-done.9), kind=kOutput, calls=%fused_computation.40 | convolution fusion | flops 2418409472 | bytes 6553728 | tf_op jit(solution)/shard_map/iftx,wsrx->iwftsr/dot_general | solution.py:82
  202.2 10.9 %copy.79 = f32[2,16,3,32,32,2]{1,5,4,3,2,0:T(2,128)} copy(f32[2,16,3,32,32,2]{3,4,2,0,5,1:T(8,128)} %fusion.24) | data formatting | bytes 1572864 | tf_op jit(solution)/shard_map/iftx,wsrx->iwftsr/transpose | solution.py:82
  213.2 5.3 copy.80
  218.5 5.4 all-to-all-start.1
  224.6 18.5 %all-to-all-done.1 = f32[2,16,6144]{2,0,1:T(2,128)} async-done(((f32[2,16,6144]{2,0,1:T(2,128)}), f32[2,16,6144]{2,0,1:T(2,128)}, u32[]{:S(2)}, u32[]{:S(2)}) %all-to-all-start.1) | async-done | bytes 786464 | tf_op jit(solution)/shard_map/all_to_all | solution.py:83
  247.9 9.8 %copy.82 = f32[2,16,3,32,32,2]{3,2,1,5,0,4:T(4,128)} copy(f32[2,16,3,32,32,2]{1,5,4,3,2,0:T(2,128)} %bitcast.189) | data formatting | bytes 1572864 | tf_op jit(solution)/shard_map/reshape | solution.py:86
  257.7 37.0 %multiply_reduce_fusion.7 = (f32[]{:T(128)}, f32[2,3,32,2,512]{4,1,3,0,2:T(4,128)S(1)}) fusion(f32[2,3,32,2,512]{4,3,2,1,0:T(2,128)} %param.11, f32[]{:T(128)} %bitcast.177, f32[32,512]{1,0:T(8,128)S(1)} %fusion.74, f32[2,16,3,32,32,2]{3,2,1,5,0,4:T(4,128)} %copy.82, f32[32,512,16,32,1,1]{1,3,2,5,4,0:T(8,128)} %bitcast.180, ...), kind=kOutput, calls=%fused_computation.74 | convolution fusion | flops 1209729024 | bytes 36765704 | tf_op jit(solution)/shard_map/lwftsr,snwt->lfsrn/dot_general | solution.py:68
  295.7 75.5 %convolution_bitcast_fusion = f32[2,16,3,32,32,2]{3,2,1,5,0,4:T(4,128)} fusion(f32[32,512,16,32,1,1]{1,3,2,5,4,0:T(8,128)} %bitcast.181, f32[2,3,32,2,512]{4,1,3,0,2:T(4,128)S(1)} %get-tuple-element.44), kind=kOutput, calls=%fused_computation.30 | convolution fusion | flops 1207959552 | bytes 35127296 | tf_op jit(solution)/shard_map/lfsrn,snwt->lwftsr/dot_general | solution.py:64
  371.2 9.5 %copy.84 = f32[2,16,3,32,32,2]{1,5,4,3,2,0:T(2,128)} copy(f32[2,16,3,32,32,2]{3,2,1,5,0,4:T(4,128)} %convolution_bitcast_fusion) | data formatting | bytes 1572864 | tf_op jit(solution)/shard_map/lfsrn,snwt->lwftsr/transpose | solution.py:64
  385.2 25.1 %all_to_all.20 = f32[2,16,6144]{2,0,1:T(2,128)} all-to-all(f32[2,16,6144]{2,0,1:T(2,128)S(1)} %copy.85), channel_id=1, replica_groups=mesh['wave'=16,'field'=2] {'wave'}, dimensions={1} | all-to-all | bytes 1572864 | tf_op jit(solution)/shard_map/all_to_all | solution.py:94
  415.2 9.6 %copy.87 = f32[2,16,3,32,32,2]{4,3,1,5,2,0:T(8,128)} copy(f32[2,16,3,32,32,2]{1,5,4,3,2,0:T(2,128)} %bitcast.191) | data formatting | bytes 1572864 | tf_op jit(solution)/shard_map/reshape | solution.py:98
  424.7 7.9 %fusion.37 = f32[2,3,32,1024]{3,2,1,0:T(8,128)S(1)} fusion(f32[2,16,3,32,32,2]{4,3,1,5,2,0:T(8,128)} %copy.87, f32[32]{0:T(128)S(1)} %dynamic_slice.7, f32[16,32,1,1024]{3,1,0,2:T(8,128)} %get-tuple-element.41, f32[16,32,1,1024]{3,1,0,2:T(8,128)} %get-tuple-element.42), kind=kOutput, calls=%fused_computation.49 | convolution fusion | flops 2418212864 | bytes 5767296 | tf_op jit(solution)/shard_map/iwftsr,wsrx->iftx/dot_general | solution.py:99
  434.8 20.4 %fusion.27 = f32[2,16,3,32,32,2]{3,4,2,0,5,1:T(8,128)S(1)} fusion(f32[2,1,3,32,1024]{4,3,1,2,0:T(8,128)S(1)} %bitcast.196, f32[2,1,3,32,1024]{4,3,1,2,0:T(8,128)S(1)} %bitcast.195, f32[16,32,2,1,1024]{4,1,0,2,3:T(8,128)S(1)} %copy-done.6, f32[16,32,2,1,1024]{4,1,0,2,3:T(8,128)S(1)} %copy-done.7), kind=kOutput, calls=%fused_computation.41 | convolution fusion | flops 4834328576 | bytes 10747904 | tf_op jit(solution)/shard_map/ikftx,wsrkx->iwftsr/dot_general | solution.py:103
  455.3 8.1 %copy.89 = f32[2,16,3,32,32,2]{1,5,4,3,2,0:T(2,128)} copy(f32[2,16,3,32,32,2]{3,4,2,0,5,1:T(8,128)S(1)} %fusion.27) | data formatting | bytes 1572864 | tf_op jit(solution)/shard_map/ikftx,wsrkx->iwftsr/transpose | solution.py:103
  472.5 8.7 %convert_multiply_fusion = f32[20,2,3,32,2,512]{5,4,3,2,1,0:T(2,128)} fusion(bf16[20,2,3,32,2,512]{5,4,3,2,1,0:T(2,128)(2,1)} %param.13, f32[32,512]{1,0:T(8,128)S(1)} %fusion.74), kind=kLoop, calls=%fused_computation.8 | loop fusion | flops 7864320 | bytes 23658496 | tf_op jit(solution)/shard_map/mul | solution.py:88
  481.9 30.3 %reshape.276 = f32[20,196608]{1,0:T(8,128)} reshape(f32[20,2,3,32,2,512]{5,4,3,2,1,0:T(2,128)} %convert_multiply_fusion) | data formatting | bytes 31457280 | tf_op jit(solution)/shard_map/reshape | solution.py:88
  512.2 29.0 %dot_general.57 = f32[2,3,32,2,512,20]{4,3,2,1,0,5:T(2,128)} reshape(f32[196608,20]{0,1:T(8,128)} %bitcast.185) | data formatting | bytes 31457280 | tf_op jit(solution)/shard_map/dot_general | solution.py:144
  541.2 43.0 %fusion.47 = f32[20,20]{1,0:T(8,128)S(1)} fusion(f32[20,2,3,32,2,512]{5,4,3,2,1,0:T(2,128)} %convert_multiply_fusion), kind=kOutput, calls=%fused_computation.59 | convolution fusion | flops 943718400 | bytes 15730240 | tf_op jit(solution)/shard_map/dot_general | solution.py:117
  588.2 9.9 %copy.92 = f32[2,16,3,32,32,2]{3,2,1,5,0,4:T(4,128)} copy(f32[2,16,3,32,32,2]{1,5,4,3,2,0:T(2,128)} %bitcast.193) | data formatting | bytes 1572864 | tf_op jit(solution)/shard_map/reshape | solution.py:107
  598.1 36.4 %fusion.42 = f32[2,3,32,2,512]{4,1,3,0,2:T(4,128)S(1)} fusion(f32[2,3,32,2,512]{4,1,3,0,2:T(4,128)} %copy-done, f32[2,16,3,32,32,2]{3,2,1,5,0,4:T(4,128)} %copy.92, f32[32,512,16,32,1,1]{1,3,2,5,4,0:T(8,128)} %bitcast.182, f32[32,512]{1,0:T(8,128)S(1)} %fusion.74), kind=kOutput, calls=%fused_computation.54 | convolution fusion | flops 1208549376 | bytes 35979264 | tf_op jit(solution)/shard_map/lwftsr,snwt->lfsrn/dot_general | solution.py:68
  636.5 22.9 %fusion.50 = f32[20]{0:T(128)S(1)} fusion(f32[20,2,3,32,2,512]{5,4,3,2,1,0:T(2,128)S(1)} %bitcast.184, f32[2,3,32,2,512,1]{4,1,3,0,2,5:T(4,128)S(1)} %bitcast.194), kind=kOutput, calls=%fused_computation.60 | convolution fusion | flops 47185920 | bytes 16515152 | tf_op jit(solution)/shard_map/dot_general | solution.py:92
  659.4 22.9 %fusion.53 = f32[20]{0:T(128)S(1)} fusion(f32[20,2,3,32,2,512]{5,4,3,2,1,0:T(2,128)S(1)} %bitcast.184, f32[2,3,32,2,512,1]{4,1,3,0,2,5:T(4,128)S(1)} %get-tuple-element.36), kind=kOutput, calls=%fused_computation.61 | convolution fusion | flops 47185920 | bytes 16515152 | tf_op jit(solution)/shard_map/dot_general | solution.py:92
  682.3 41.9 %all-reduce = (f32[]{:T(128)}, f32[20]{0:T(128)S(1)}, f32[20]{0:T(128)S(1)}, f32[]{:T(128)}, f32[]{:T(128)}, /*index=5*/f32[]{:T(128)}, f32[20,20]{1,0:T(8,128)S(1)}) all-reduce(f32[]{:T(128)} %get-tuple-element.43, f32[20]{0:T(128)S(1)} %fusion.53, f32[20]{0:T(128)S(1)} %fusion.50, ...), channel_id=1, replica_groups=mesh['wave'=16,'field'=2] {'wave','field'}, use_global_device_ids=true, to_apply=%region_3.4 | all-reduce | flops 444 | bytes 3552 | tf_op jit(solution)/shard_map/psum | solution.py:109
  731.2 24.4 %fusion.6 = f32[1,2,3,32,2,512]{5,0,4,3,2,1:T(1,128)S(1)} fusion(f32[2,3,32,2,512,20]{4,3,2,1,0,5:T(2,128)} %dot_general.57, f32[20]{0:T(128)S(1)} %get-tuple-element.33), kind=kOutput, calls=%fused_computation.6 | convolution fusion | flops 47185920 | bytes 16515152 | tf_op jit(solution)/shard_map/dot_general | solution.py:144
  (65 shorter events, 56.7 us)
Async XLA Ops:
  1.5 33.4 %copy-start.1 = (f32[2,3,32,2,512]{4,3,2,1,0:T(2,128)S(1)}, f32[2,3,32,2,512]{4,3,2,1,0:T(2,128)}, u32[]{:S(2)}) copy-start(f32[2,3,32,2,512]{4,3,2,1,0:T(2,128)} %param.10) | copy-start | bytes 2359300
  130.7 13.8 %copy-start.11 = (s32[512]{0:T(512)S(1)}, s32[512]{0:T(512)}, u32[]{:S(2)}) copy-start(s32[512]{0:T(512)} %param.15) | copy-start | bytes 6148
  130.7 13.9 %copy-start.10 = (bf16[3,3,32,1024]{3,2,1,0:T(8,128)(2,1)S(1)}, bf16[3,3,32,1024]{3,2,1,0:T(8,128)(2,1)}, u32[]{:S(2)}) copy-start(bf16[3,3,32,1024]{3,2,1,0:T(8,128)(2,1)} %param.18) | copy-start | bytes 1769476
  136.1 28.1 %all-to-all-start = ((f32[2,16,6144]{2,0,1:T(2,128)}), f32[2,16,6144]{2,0,1:T(2,128)}, u32[]{:S(2)}, u32[]{:S(2)}) async-start(f32[2,16,6144]{2,0,1:T(2,128)} %copy.75), calls=%async_computation | async-start | bytes 1572864 | tf_op jit(solution)/shard_map/all_to_all | solution.py:73
  188.3 1.6 copy-start.8
  188.3 2.2 copy-start.9
  218.5 24.5 %all-to-all-start.1 = ((f32[2,16,6144]{2,0,1:T(2,128)}), f32[2,16,6144]{2,0,1:T(2,128)}, u32[]{:S(2)}, u32[]{:S(2)}) async-start(f32[2,16,6144]{2,0,1:T(2,128)} %copy.80), calls=%async_computation.1 | async-start | bytes 1572864 | tf_op jit(solution)/shard_map/all_to_all | solution.py:83
  294.7 1.0 copy-start
  424.7 8.4 %copy-start.7 = (f32[16,32,2,1,1024]{4,1,0,2,3:T(8,128)S(1)}, f32[16,32,2,1,1024]{4,1,0,2,3:T(8,128)}, u32[]{:S(2)}) copy-start(f32[16,32,2,1,1024]{4,1,0,2,3:T(8,128)} %fusion.14) | copy-start | bytes 12582916
  432.7 2.2 copy-start.6
  468.8 115.4 %all-to-all-start.3 = ((f32[2,16,6144]{2,0,1:T(2,128)}), f32[2,16,6144]{2,0,1:T(2,128)S(1)}, u32[]{:S(2)}, u32[]{:S(2)}) async-start(f32[2,16,6144]{2,0,1:T(2,128)} %copy.90), calls=%async_computation.3 | async-start | bytes 1572864 | tf_op jit(solution)/shard_map/all_to_all | solution.py:104
  588.2 48.3 %slice-start = ((s8[15728640]{0:T(1024)(128)(4,1)}), s8[3145728]{0:T(1024)(128)(4,1)S(1)}, s32[]{:S(2)}) async-start(s8[15728640]{0:T(1024)(128)(4,1)} %bitcast.183), calls=%async_computation.4 | async-start | bytes 6291456
  598.1 36.4 %copy-start.2 = (f32[2,3,32,2,512]{4,3,2,1,0:T(2,128)S(1)}, f32[2,3,32,2,512]{4,3,2,1,0:T(2,128)}, u32[]{:S(2)}) copy-start(f32[2,3,32,2,512]{4,3,2,1,0:T(2,128)} %param.10) | copy-start | bytes 2359300
  598.1 38.4 %slice-start.1 = ((s8[15728640]{0:T(1024)(128)(4,1)}), s8[4194304]{0:T(1024)(128)(4,1)S(1)}, s32[]{:S(2)}) async-start(s8[15728640]{0:T(1024)(128)(4,1)} %bitcast.183), calls=%async_computation.5 | async-start | bytes 8388608
  598.1 38.4 %slice-start.2 = ((s8[15728640]{0:T(1024)(128)(4,1)}), s8[4194304]{0:T(1024)(128)(4,1)S(1)}, s32[]{:S(2)}) async-start(s8[15728640]{0:T(1024)(128)(4,1)} %bitcast.183), calls=%async_computation.6 | async-start | bytes 8388608
  598.1 38.4 %slice-start.3 = ((s8[15728640]{0:T(1024)(128)(4,1)}), s8[4194304]{0:T(1024)(128)(4,1)S(1)}, s32[]{:S(2)}) async-start(s8[15728640]{0:T(1024)(128)(4,1)} %bitcast.183), calls=%async_computation.7 | async-start | bytes 8388608
  634.6 24.8 %copy-start.4 = (f32[2,3,32,2,512]{4,1,3,0,2:T(4,128)}, f32[2,3,32,2,512]{4,1,3,0,2:T(4,128)S(1)}, u32[]{:S(2)}) copy-start(f32[2,3,32,2,512]{4,1,3,0,2:T(4,128)S(1)} %fusion.42) | copy-start | bytes 2359300
  728.4 27.2 %copy-start.12 = (f32[20]{0:T(128)}, f32[20]{0:T(128)S(1)}, u32[]{:S(2)}) copy-start(f32[20]{0:T(128)S(1)} %get-tuple-element.33) | copy-start | bytes 244
  731.1 24.5 %copy-start.3 = (f32[2,3,32,2,512]{4,3,2,1,0:T(2,128)S(1)}, f32[2,3,32,2,512]{4,3,2,1,0:T(2,128)}, u32[]{:S(2)}) copy-start(f32[2,3,32,2,512]{4,3,2,1,0:T(2,128)} %param.10) | copy-start | bytes 2359300
  731.2 24.5 %copy-start.5 = (f32[2,3,32,2,512]{4,1,3,0,2:T(4,128)S(1)}, f32[2,3,32,2,512]{4,1,3,0,2:T(4,128)}, u32[]{:S(2)}) copy-start(f32[2,3,32,2,512]{4,1,3,0,2:T(4,128)} %copy-done.4) | copy-start | bytes 2359300
where the time goes:
time: 773 us; the launch traced here: 761 us
  matrix products  399 us (52%)
  local copies, waits for them, and re-layouts  217 us (28%)
  blocking collectives  67.1 us (9%)
  other arithmetic  32.5 us (4%)
  waiting for transfers between devices  20.4 us (3%)
  starting transfers between devices  17.6 us (2%)
    dot_general x2, matrix products, to_latitudes(): jnp.einsum('lfsrn,snwt->lwftsr', spectral, blocked, precision=highest)  162 us
    dot_general x2, matrix products, to_degrees(): jnp.einsum('lwftsr,snwt->lfsrn', gathered, blocked, precision=highest)  73.4 us
    dot_general x2, matrix products, project(): return jnp.dot(kept_live, vector.reshape(-1), precision=highest)  45.8 us
    dot_general x1, matrix products, body(): jnp.dot(kept_live, kept_live.T, precision=highest)  43 us
    psum x1, blocking collectives, body(): lax.psum((jnp.sum(residual_left * residual_left), jnp.sum(adjoint_raw * a...  41.9 us
    unnamed x37, local copies, waits for them, and re-layouts  40.2 us
    reshape x1, local copies, waits for them, and re-layouts, body(): (kept_vectors.astype(jnp.float32) * wide_mask[None]).reshape(keep_count, -1)  30.3 us
    dot_general x1, local copies, waits for them, and re-layouts, body(): jnp.dot(correlations, kept_live, precision=highest)  29 us
  transfers between devices with their start and end apart: 3, of which 2 were waited for; matrix products, arithmetic and copies ran while one was open for 17% of the time, Pallas kernels for 0%

commit v1 on v0

--- a/solution.py
+++ b/solution.py
@@ -107,16 +107,19 @@
     gathered = returned.reshape(item_count, groups, fields, lat_dev, waves_dev, 2)
     adjoint_raw = residual_left + time_step * to_degrees(gathered)
     totals = lax.psum(
-        (
-            jnp.sum(residual_left * residual_left),
-            jnp.sum(adjoint_raw * adjoint_raw),
-            jnp.sum(adjoint_raw * right_live),
-            jnp.sum(right_live * right_live),
-            project(adjoint_raw),
-            project(right_live),
-            jnp.dot(kept_live, kept_live.T, precision=highest),
+        lax.psum(
+            (
+                jnp.sum(residual_left * residual_left),
+                jnp.sum(adjoint_raw * adjoint_raw),
+                jnp.sum(adjoint_raw * right_live),
+                jnp.sum(right_live * right_live),
+                project(adjoint_raw),
+                project(right_live),
+                jnp.dot(kept_live, kept_live.T, precision=highest),
+            ),
+            "field",
         ),
-        ("wave", "field"),
+        "wave",
     )
     left_square, image_square, image_cross, right_square, kept_image, kept_right, gram_matrix = [
         summed / entries for summed in totals

time: 773 us -> 814 us (1.053)
  blocking collectives: 67.1 us -> 107 us
    psum x0 -> x1, blocking collectives: none -> 77.2 us  [body(): lax.psum(lax.psum((jnp.sum(residual_left * residual_left), jnp.sum(adjoin...]
    psum x1, blocking collectives: 41.9 us -> 4.51 us  [body(): lax.psum((jnp.sum(residual_left * residual_left), jnp.sum(adjoint_raw * a...]
  transfers between devices with their start and end apart: 3 -> 3, of which waited for: 2 -> 2; matrix products, arithmetic and copies ran while one was open for 17% -> 16% of each run, Pallas kernels for 0% -> 0%
where the time goes in v1:
time: 814 us; the launch traced here: 801 us
  matrix products  400 us (49%)
  local copies, waits for them, and re-layouts  217 us (27%)
  blocking collectives  107 us (13%)
  other arithmetic  32.6 us (4%)
  waiting for transfers between devices  20.4 us (3%)
  starting transfers between devices  17.6 us (2%)
    dot_general x2, matrix products, to_latitudes(): jnp.einsum('lfsrn,snwt->lwftsr', spectral, blocked, precision=highest)  162 us
    psum x1, blocking collectives, body(): lax.psum(lax.psum((jnp.sum(residual_left * residual_left), jnp.sum(adjoin...  77.2 us
    dot_general x2, matrix products, to_degrees(): jnp.einsum('lwftsr,snwt->lfsrn', gathered, blocked, precision=highest)  73.4 us
    dot_general x2, matrix products, project(): return jnp.dot(kept_live, vector.reshape(-1), precision=highest)  45.8 us
    dot_general x1, matrix products, body(): jnp.dot(kept_live, kept_live.T, precision=highest)  43.9 us
    unnamed x37, local copies, waits for them, and re-layouts  40.2 us
    reshape x1, local copies, waits for them, and re-layouts, body(): (kept_vectors.astype(jnp.float32) * wide_mask[None]).reshape(keep_count, -1)  30.4 us
    dot_general x1, local copies, waits for them, and re-layouts, body(): jnp.dot(correlations, kept_live, precision=highest)  29 us
  transfers between devices with their start and end apart: 3, of which 2 were waited for; matrix products, arithmetic and copies ran while one was open for 16% of the time, Pallas kernels for 0%

profile of v1, /device:TPU:0, one launch (start us, length us, event | category | flops | bytes accessed | tf_op | source)
XLA Modules:
  0.0 801.1 jit_solution(1283704664223622971)
XLA Ops:
  1.5 33.4 %copy.73 = f32[32,512,512]{1,2,0:T(8,128)} copy(f32[32,512,512]{2,1,0:T(8,128)} %param.16) | data formatting | bytes 67108864 | tf_op args[6]
  34.9 86.3 %convolution_bitcast_fusion.1 = f32[2,16,3,32,32,2]{3,2,1,5,0,4:T(4,128)} fusion(f32[32,512,16,32,1,1]{1,3,2,5,4,0:T(8,128)} %bitcast.179, f32[2,3,32,2,512]{4,3,2,1,0:T(2,128)S(1)} %copy-done.1, f32[32,512]{1,0:T(8,128)S(1)} %fusion.74), kind=kOutput, calls=%fused_computation.31 | convolution fusion | flops 1208156160 | bytes 35192832 | tf_op jit(solution)/shard_map/lfsrn,snwt->lwftsr/dot_general | solution.py:64
  121.2 9.5 %copy.74 = f32[2,16,3,32,32,2]{1,5,4,3,2,0:T(2,128)} copy(f32[2,16,3,32,32,2]{3,2,1,5,0,4:T(4,128)} %convolution_bitcast_fusion.1) | data formatting | bytes 1572864 | tf_op jit(solution)/shard_map/lfsrn,snwt->lwftsr/transpose | solution.py:64
  130.7 5.4 copy.75
  136.1 8.4 %all-to-all-start = ((f32[2,16,6144]{2,0,1:T(2,128)}), f32[2,16,6144]{2,0,1:T(2,128)}, u32[]{:S(2)}, u32[]{:S(2)}) async-start(f32[2,16,6144]{2,0,1:T(2,128)} %copy.75), calls=%async_computation | async-start | bytes 1572864 | tf_op jit(solution)/shard_map/all_to_all | solution.py:73
  146.7 10.7 %fusion.62 = (f32[16,32,1,1,1024]{4,1,0,3,2:T(8,128)S(1)}, f32[16,32,1,1,1024]{4,1,0,3,2:T(8,128)S(1)}, f32[16,32,1,1,1024]{4,1,0,2,3:T(8,128)S(1)}, f32[16,32,1...) fusion(s32[16,32]{1,0:T(8,128)S(1)} %mul.312), kind=kLoop, calls=%fused_computation.76 | loop fusion | flops 8388608 | bytes 12584960 | tf_op jit(solution)/shard_map/stack | solution.py:23
  169.1 9.5 %copy.77 = f32[2,16,3,32,32,2]{4,3,1,5,2,0:T(8,128)} copy(f32[2,16,3,32,32,2]{1,5,4,3,2,0:T(2,128)} %bitcast.187) | data formatting | bytes 1572864 | tf_op jit(solution)/shard_map/reshape | solution.py:77
  178.6 9.6 %fusion.32 = f32[2,2,3,32,1024]{4,3,2,0,1:T(8,128)S(1)} fusion(f32[2,16,3,32,32,2]{4,3,1,5,2,0:T(8,128)} %copy.77, f32[16,32,2,1,1024]{4,1,0,2,3:T(8,128)} %maximum_multiply_fusion.2, f32[16,32,2,1,1024]{4,1,0,2,3:T(8,128)} %fusion.14), kind=kOutput, calls=%fused_computation.45 | convolution fusion | flops 4833935360 | bytes 10747904 | tf_op jit(solution)/shard_map/iwftsr,wsrkx->ikftx/dot_general | solution.py:78
  190.4 11.7 %fusion.24 = f32[2,16,3,32,32,2]{3,4,2,0,5,1:T(8,128)} fusion(f32[2,3,32,1024]{3,2,1,0:T(8,128)S(1)} %get-tuple-element.53, f32[2,3,32,1024]{3,2,1,0:T(8,128)S(1)} %get-tuple-element.52, f32[32]{0:T(128)S(1)} %dynamic_slice.7, f32[16,32,1,1024]{3,1,0,2:T(8,128)S(1)} %copy-done.8, f32[16,32,1,1024]{3,1,0,2:T(8,128)S(1)} %copy-done.9), kind=kOutput, calls=%fused_computation.40 | convolution fusion | flops 2418409472 | bytes 6553728 | tf_op jit(solution)/shard_map/iftx,wsrx->iwftsr/dot_general | solution.py:82
  202.2 11.0 %copy.79 = f32[2,16,3,32,32,2]{1,5,4,3,2,0:T(2,128)} copy(f32[2,16,3,32,32,2]{3,4,2,0,5,1:T(8,128)} %fusion.24) | data formatting | bytes 1572864 | tf_op jit(solution)/shard_map/iftx,wsrx->iwftsr/transpose | solution.py:82
  218.4 5.4 all-to-all-start.1
  224.5 18.5 %all-to-all-done.1 = f32[2,16,6144]{2,0,1:T(2,128)} async-done(((f32[2,16,6144]{2,0,1:T(2,128)}), f32[2,16,6144]{2,0,1:T(2,128)}, u32[]{:S(2)}, u32[]{:S(2)}) %all-to-all-start.1) | async-done | bytes 786464 | tf_op jit(solution)/shard_map/all_to_all | solution.py:83
  247.9 9.8 %copy.82 = f32[2,16,3,32,32,2]{3,2,1,5,0,4:T(4,128)} copy(f32[2,16,3,32,32,2]{1,5,4,3,2,0:T(2,128)} %bitcast.189) | data formatting | bytes 1572864 | tf_op jit(solution)/shard_map/reshape | solution.py:86
  257.6 37.0 %multiply_reduce_fusion.7 = (f32[]{:T(128)}, f32[2,3,32,2,512]{4,1,3,0,2:T(4,128)S(1)}) fusion(f32[2,3,32,2,512]{4,3,2,1,0:T(2,128)} %param.11, f32[]{:T(128)} %bitcast.177, f32[32,512]{1,0:T(8,128)S(1)} %fusion.74, f32[2,16,3,32,32,2]{3,2,1,5,0,4:T(4,128)} %copy.82, f32[32,512,16,32,1,1]{1,3,2,5,4,0:T(8,128)} %bitcast.180, ...), kind=kOutput, calls=%fused_computation.74 | convolution fusion | flops 1209729024 | bytes 36765704 | tf_op jit(solution)/shard_map/lwftsr,snwt->lfsrn/dot_general | solution.py:68
  295.6 75.5 %convolution_bitcast_fusion = f32[2,16,3,32,32,2]{3,2,1,5,0,4:T(4,128)} fusion(f32[32,512,16,32,1,1]{1,3,2,5,4,0:T(8,128)} %bitcast.181, f32[2,3,32,2,512]{4,1,3,0,2:T(4,128)S(1)} %get-tuple-element.51), kind=kOutput, calls=%fused_computation.30 | convolution fusion | flops 1207959552 | bytes 35127296 | tf_op jit(solution)/shard_map/lfsrn,snwt->lwftsr/dot_general | solution.py:64
  371.1 9.5 %copy.84 = f32[2,16,3,32,32,2]{1,5,4,3,2,0:T(2,128)} copy(f32[2,16,3,32,32,2]{3,2,1,5,0,4:T(4,128)} %convolution_bitcast_fusion) | data formatting | bytes 1572864 | tf_op jit(solution)/shard_map/lfsrn,snwt->lwftsr/transpose | solution.py:64
  385.1 25.1 %all_to_all.20 = f32[2,16,6144]{2,0,1:T(2,128)} all-to-all(f32[2,16,6144]{2,0,1:T(2,128)S(1)} %copy.85), channel_id=1, replica_groups=mesh['wave'=16,'field'=2] {'wave'}, dimensions={1} | all-to-all | bytes 1572864 | tf_op jit(solution)/shard_map/all_to_all | solution.py:94
  415.1 9.5 %copy.87 = f32[2,16,3,32,32,2]{4,3,1,5,2,0:T(8,128)} copy(f32[2,16,3,32,32,2]{1,5,4,3,2,0:T(2,128)} %bitcast.191) | data formatting | bytes 1572864 | tf_op jit(solution)/shard_map/reshape | solution.py:98
  424.6 7.9 fusion.37
  434.8 20.4 %fusion.27 = f32[2,16,3,32,32,2]{3,4,2,0,5,1:T(8,128)S(1)} fusion(f32[2,1,3,32,1024]{4,3,1,2,0:T(8,128)S(1)} %bitcast.196, f32[2,1,3,32,1024]{4,3,1,2,0:T(8,128)S(1)} %bitcast.195, f32[16,32,2,1,1024]{4,1,0,2,3:T(8,128)S(1)} %copy-done.6, f32[16,32,2,1,1024]{4,1,0,2,3:T(8,128)S(1)} %copy-done.7), kind=kOutput, calls=%fused_computation.41 | convolution fusion | flops 4834328576 | bytes 10747904 | tf_op jit(solution)/shard_map/ikftx,wsrkx->iwftsr/dot_general | solution.py:103
  455.2 8.2 %copy.89 = f32[2,16,3,32,32,2]{1,5,4,3,2,0:T(2,128)} copy(f32[2,16,3,32,32,2]{3,4,2,0,5,1:T(8,128)S(1)} %fusion.27) | data formatting | bytes 1572864 | tf_op jit(solution)/shard_map/ikftx,wsrkx->iwftsr/transpose | solution.py:103
  463.4 5.3 copy.90
  472.5 8.7 %convert_multiply_fusion = f32[20,2,3,32,2,512]{5,4,3,2,1,0:T(2,128)} fusion(bf16[20,2,3,32,2,512]{5,4,3,2,1,0:T(2,128)(2,1)} %param.13, f32[32,512]{1,0:T(8,128)S(1)} %fusion.74), kind=kLoop, calls=%fused_computation.8 | loop fusion | flops 7864320 | bytes 23658496 | tf_op jit(solution)/shard_map/mul | solution.py:88
  481.8 30.4 %reshape.276 = f32[20,196608]{1,0:T(8,128)} reshape(f32[20,2,3,32,2,512]{5,4,3,2,1,0:T(2,128)} %convert_multiply_fusion) | data formatting | bytes 31457280 | tf_op jit(solution)/shard_map/reshape | solution.py:88
  512.2 29.0 %dot_general.57 = f32[2,3,32,2,512,20]{4,3,2,1,0,5:T(2,128)} reshape(f32[196608,20]{0,1:T(8,128)} %bitcast.185) | data formatting | bytes 31457280 | tf_op jit(solution)/shard_map/dot_general | solution.py:147
  541.2 43.9 %fusion.47 = f32[20,20]{1,0:T(8,128)S(1)} fusion(f32[20,2,3,32,2,512]{5,4,3,2,1,0:T(2,128)} %convert_multiply_fusion), kind=kOutput, calls=%fused_computation.59 | convolution fusion | flops 943718400 | bytes 15730240 | tf_op jit(solution)/shard_map/dot_general | solution.py:118
  589.0 9.9 %copy.92 = f32[2,16,3,32,32,2]{3,2,1,5,0,4:T(4,128)} copy(f32[2,16,3,32,32,2]{1,5,4,3,2,0:T(2,128)} %bitcast.193) | data formatting | bytes 1572864 | tf_op jit(solution)/shard_map/reshape | solution.py:107
  599.0 36.4 %fusion.42 = f32[2,3,32,2,512]{4,1,3,0,2:T(4,128)S(1)} fusion(f32[2,3,32,2,512]{4,1,3,0,2:T(4,128)} %copy-done, f32[2,16,3,32,32,2]{3,2,1,5,0,4:T(4,128)} %copy.92, f32[32,512,16,32,1,1]{1,3,2,5,4,0:T(8,128)} %bitcast.182, f32[32,512]{1,0:T(8,128)S(1)} %fusion.74), kind=kOutput, calls=%fused_computation.54 | convolution fusion | flops 1208549376 | bytes 35979264 | tf_op jit(solution)/shard_map/lwftsr,snwt->lfsrn/dot_general | solution.py:68
  637.3 22.9 %fusion.50 = f32[20]{0:T(128)S(1)} fusion(f32[20,2,3,32,2,512]{5,4,3,2,1,0:T(2,128)S(1)} %bitcast.184, f32[2,3,32,2,512,1]{4,1,3,0,2,5:T(4,128)S(1)} %bitcast.194), kind=kOutput, calls=%fused_computation.60 | convolution fusion | flops 47185920 | bytes 16515152 | tf_op jit(solution)/shard_map/dot_general | solution.py:92
  660.2 22.9 %fusion.53 = f32[20]{0:T(128)S(1)} fusion(f32[20,2,3,32,2,512]{5,4,3,2,1,0:T(2,128)S(1)} %bitcast.184, f32[2,3,32,2,512,1]{4,1,3,0,2,5:T(4,128)S(1)} %get-tuple-element.43), kind=kOutput, calls=%fused_computation.61 | convolution fusion | flops 47185920 | bytes 16515152 | tf_op jit(solution)/shard_map/dot_general | solution.py:92
  687.6 77.2 %all-reduce = (f32[]{:T(128)}, f32[20]{0:T(128)S(1)}, f32[20]{0:T(128)S(1)}, f32[]{:T(128)}, f32[]{:T(128)}, /*index=5*/f32[]{:T(128)}, f32[20,20]{1,0:T(8,128)S(1)}) all-reduce(f32[]{:T(128)} %get-tuple-element.32, f32[20]{0:T(128)S(1)} %get-tuple-element.33, ...), channel_id=1, replica_groups=mesh['wave'=16,'field'=2] {'wave'}, use_global_device_ids=true, to_apply=%region_4.5 | all-reduce | flops 444 | bytes 3552 | tf_op jit(solution)/shard_map/psum | solution.py:109
  771.7 24.4 %fusion.6 = f32[1,2,3,32,2,512]{5,0,4,3,2,1:T(1,128)S(1)} fusion(f32[2,3,32,2,512,20]{4,3,2,1,0,5:T(2,128)} %dot_general.57, f32[20]{0:T(128)S(1)} %get-tuple-element.40), kind=kOutput, calls=%fused_computation.6 | convolution fusion | flops 47185920 | bytes 16515152 | tf_op jit(solution)/shard_map/dot_general | solution.py:147
  (66 shorter events, 61.1 us)
Async XLA Ops:
  1.5 33.4 %copy-start.1 = (f32[2,3,32,2,512]{4,3,2,1,0:T(2,128)S(1)}, f32[2,3,32,2,512]{4,3,2,1,0:T(2,128)}, u32[]{:S(2)}) copy-start(f32[2,3,32,2,512]{4,3,2,1,0:T(2,128)} %param.10) | copy-start | bytes 2359300
  130.7 13.8 %copy-start.11 = (s32[512]{0:T(512)S(1)}, s32[512]{0:T(512)}, u32[]{:S(2)}) copy-start(s32[512]{0:T(512)} %param.15) | copy-start | bytes 6148
  130.7 13.9 %copy-start.10 = (bf16[3,3,32,1024]{3,2,1,0:T(8,128)(2,1)S(1)}, bf16[3,3,32,1024]{3,2,1,0:T(8,128)(2,1)}, u32[]{:S(2)}) copy-start(bf16[3,3,32,1024]{3,2,1,0:T(8,128)(2,1)} %param.18) | copy-start | bytes 1769476
  136.1 28.1 %all-to-all-start = ((f32[2,16,6144]{2,0,1:T(2,128)}), f32[2,16,6144]{2,0,1:T(2,128)}, u32[]{:S(2)}, u32[]{:S(2)}) async-start(f32[2,16,6144]{2,0,1:T(2,128)} %copy.75), calls=%async_computation | async-start | bytes 1572864 | tf_op jit(solution)/shard_map/all_to_all | solution.py:73
  188.2 1.6 copy-start.8
  188.2 2.2 copy-start.9
  218.4 24.6 %all-to-all-start.1 = ((f32[2,16,6144]{2,0,1:T(2,128)}), f32[2,16,6144]{2,0,1:T(2,128)}, u32[]{:S(2)}, u32[]{:S(2)}) async-start(f32[2,16,6144]{2,0,1:T(2,128)} %copy.80), calls=%async_computation.1 | async-start | bytes 1572864 | tf_op jit(solution)/shard_map/all_to_all | solution.py:83
  294.6 1.0 copy-start
  424.6 8.4 %copy-start.7 = (f32[16,32,2,1,1024]{4,1,0,2,3:T(8,128)S(1)}, f32[16,32,2,1,1024]{4,1,0,2,3:T(8,128)}, u32[]{:S(2)}) copy-start(f32[16,32,2,1,1024]{4,1,0,2,3:T(8,128)} %fusion.14) | copy-start | bytes 12582916
  432.6 2.2 copy-start.6
  468.7 116.3 %all-to-all-start.3 = ((f32[2,16,6144]{2,0,1:T(2,128)}), f32[2,16,6144]{2,0,1:T(2,128)S(1)}, u32[]{:S(2)}, u32[]{:S(2)}) async-start(f32[2,16,6144]{2,0,1:T(2,128)} %copy.90), calls=%async_computation.3 | async-start | bytes 1572864 | tf_op jit(solution)/shard_map/all_to_all | solution.py:104
  589.0 48.3 %slice-start = ((s8[15728640]{0:T(1024)(128)(4,1)}), s8[3145728]{0:T(1024)(128)(4,1)S(1)}, s32[]{:S(2)}) async-start(s8[15728640]{0:T(1024)(128)(4,1)} %bitcast.183), calls=%async_computation.4 | async-start | bytes 6291456
  599.0 36.4 %copy-start.2 = (f32[2,3,32,2,512]{4,3,2,1,0:T(2,128)S(1)}, f32[2,3,32,2,512]{4,3,2,1,0:T(2,128)}, u32[]{:S(2)}) copy-start(f32[2,3,32,2,512]{4,3,2,1,0:T(2,128)} %param.10) | copy-start | bytes 2359300
  599.0 38.4 %slice-start.1 = ((s8[15728640]{0:T(1024)(128)(4,1)}), s8[4194304]{0:T(1024)(128)(4,1)S(1)}, s32[]{:S(2)}) async-start(s8[15728640]{0:T(1024)(128)(4,1)} %bitcast.183), calls=%async_computation.5 | async-start | bytes 8388608
  599.0 38.4 %slice-start.2 = ((s8[15728640]{0:T(1024)(128)(4,1)}), s8[4194304]{0:T(1024)(128)(4,1)S(1)}, s32[]{:S(2)}) async-start(s8[15728640]{0:T(1024)(128)(4,1)} %bitcast.183), calls=%async_computation.6 | async-start | bytes 8388608
  599.0 38.4 %slice-start.3 = ((s8[15728640]{0:T(1024)(128)(4,1)}), s8[4194304]{0:T(1024)(128)(4,1)S(1)}, s32[]{:S(2)}) async-start(s8[15728640]{0:T(1024)(128)(4,1)} %bitcast.183), calls=%async_computation.7 | async-start | bytes 8388608
  635.4 24.8 %copy-start.4 = (f32[2,3,32,2,512]{4,1,3,0,2:T(4,128)}, f32[2,3,32,2,512]{4,1,3,0,2:T(4,128)S(1)}, u32[]{:S(2)}) copy-start(f32[2,3,32,2,512]{4,1,3,0,2:T(4,128)S(1)} %fusion.42) | copy-start | bytes 2359300
  769.0 27.2 %copy-start.12 = (f32[20]{0:T(128)}, f32[20]{0:T(128)S(1)}, u32[]{:S(2)}) copy-start(f32[20]{0:T(128)S(1)} %get-tuple-element.40) | copy-start | bytes 244
  771.7 24.5 %copy-start.3 = (f32[2,3,32,2,512]{4,3,2,1,0:T(2,128)S(1)}, f32[2,3,32,2,512]{4,3,2,1,0:T(2,128)}, u32[]{:S(2)}) copy-start(f32[2,3,32,2,512]{4,3,2,1,0:T(2,128)} %param.10) | copy-start | bytes 2359300
  771.7 24.5 %copy-start.5 = (f32[2,3,32,2,512]{4,1,3,0,2:T(4,128)S(1)}, f32[2,3,32,2,512]{4,1,3,0,2:T(4,128)}, u32[]{:S(2)}) copy-start(f32[2,3,32,2,512]{4,1,3,0,2:T(4,128)} %copy-done.4) | copy-start | bytes 2359300
